TPU v7x, 32 devices: a whole 2x2x4 slice. The times are simulated.
32 devices in a mesh: prow: 16 (over z, y, x), pcol: 2 (over core).
Axes of the slice: x: 2, y: 2, z: 4, core: 2. Of those that a mesh axis runs over, the one named last changes fastest.
Arguments:
- right_sides: float32 [32, 1, 4096], P(None, None, 'prow'), may hold values from -6 to 6
- factor: bfloat16 [1, 4096, 8, 512], P(None, 'prow', None, 'pcol'), as said below
- node_sizes: int32 [7], replicated, may hold values from 1 to 9, 16 in all
- row_blocks: int32 [7, 16], replicated, may hold values 0 or 1
Outputs:
- forward: float32 [32, 1, 4096], P(None, None, 'prow')
- solution: float32 [32, 8, 512], P(None, None, 'pcol')
Inputs may be any that keep to these rules, and one draw needn't show every extreme that they name: factor is zero above its diagonal; its diagonal lies between 0.5 and 1. `row_blocks`: flags of tiles that belong to no proper ancestor of the supernode are ignored.
All inputs are finite; a program needn't handle non-finite values.
Results may differ from a plain program's by a relative error of at most 0.0047.
Values may be sent and summed in bfloat16 or wider, within the bound.
A program may use at most 64 MiB of HBM per device.

v0:
```python
import jax
import jax.numpy as jnp
from jax import lax
from jax.sharding import PartitionSpec as P

LEVELS = 3


def tree_tables(node_sizes, row_blocks):
    node_count = node_sizes.shape[0]
    tile_count = row_blocks.shape[1]
    tile_ends = jnp.cumsum(node_sizes)
    tile_ids = jnp.arange(tile_count, dtype=jnp.int32)
    node_of = jnp.sum((tile_ends[None, :] <= tile_ids[:, None]).astype(jnp.int32), axis=1)
    heap_label = node_count - jnp.arange(node_count, dtype=jnp.int32)
    node_depth = jnp.zeros((node_count,), jnp.int32)
    for exponent in range(1, LEVELS):
        node_depth = node_depth + (heap_label >= 2**exponent).astype(jnp.int32)
    gap_depth = jnp.maximum(node_depth[None, :] - node_depth[:, None], 0)
    ancestor = (node_depth[:, None] < node_depth[None, :]) & (
        jnp.right_shift(heap_label[None, :], gap_depth) == heap_label[:, None]
    )
    return (node_of, node_depth, ancestor)


def lookup(source, indices, length):
    hits = indices[:, None] == jnp.arange(length, dtype=jnp.int32)[None, :]
    return jnp.sum(jnp.where(hits, source[None, :], 0), axis=1)


def rows_from_columns(factor, vector, weights):
    blocks = lax.dot_general(
        vector, factor, (((2,), (3,)), ((1,), (2,))), preferred_element_type=jnp.float32
    )
    return jnp.sum(weights.T[:, None, :, None] * blocks, axis=0)


def columns_from_rows(factor, vector, weights):
    blocks = lax.dot_general(
        vector, factor, (((2,), (1,)), ((1,), (0,))), preferred_element_type=jnp.float32
    )
    return jnp.sum(weights[:, None, :, None] * blocks, axis=0)


def to_columns(vector):
    row_count = lax.axis_size("prow")
    col_count = lax.axis_size("pcol")
    row_groups = row_count // col_count
    col_index = lax.axis_index("pcol")
    rhs_count, row_tiles, tile_rows = vector.shape
    collected = lax.all_gather(vector, "prow", axis=1, tiled=True)
    collected = collected.reshape(rhs_count, row_groups, col_count, row_tiles, tile_rows)
    picked = lax.dynamic_index_in_dim(collected, col_index, 2, keepdims=False)
    return jnp.transpose(picked, (0, 2, 1, 3)).reshape(rhs_count, row_tiles * row_groups, tile_rows)


def to_rows(vector):
    row_count = lax.axis_size("prow")
    col_count = lax.axis_size("pcol")
    row_groups = row_count // col_count
    row_index = lax.axis_index("prow")
    rhs_count, col_tiles, tile_rows = vector.shape
    shaped = vector.reshape(rhs_count, col_tiles // row_groups, row_groups, tile_rows)
    chosen = lax.dynamic_index_in_dim(shaped, row_index // col_count, 2, keepdims=False)
    collected = lax.all_gather(chosen, "pcol", axis=1, tiled=True)
    collected = collected.reshape(rhs_count, col_count, col_tiles // row_groups, tile_rows)
    return lax.dynamic_index_in_dim(collected, row_index % col_count, 1, keepdims=False)


def sum_rows(partial_value):
    return lax.psum(partial_value, "pcol")


def sum_cols(partial_value):
    return lax.psum(partial_value, "prow")


def shards(right_sides, factor, node_sizes, row_blocks):
    row_count = lax.axis_size("prow")
    col_count = lax.axis_size("pcol")
    row_index = lax.axis_index("prow")
    col_index = lax.axis_index("pcol")
    row_tiles = factor.shape[0]
    col_tiles = factor.shape[2]
    rhs_count = right_sides.shape[0]
    tile_rows = right_sides.shape[2]
    node_count = node_sizes.shape[0]
    tile_count = row_blocks.shape[1]
    node_of, node_depth, ancestor = tree_tables(node_sizes, row_blocks)
    mine_rows = jnp.arange(row_tiles, dtype=jnp.int32) * row_count + row_index
    mine_cols = jnp.arange(col_tiles, dtype=jnp.int32) * col_count + col_index
    owner_rows = lookup(node_of, mine_rows, tile_count)
    owner_cols = lookup(node_of, mine_cols, tile_count)
    depth_rows = lookup(node_depth, owner_rows, node_count)
    depth_cols = lookup(node_depth, owner_cols, node_count)
    node_ids = jnp.arange(node_count, dtype=jnp.int32)
    hits_rows = owner_rows[:, None] == node_ids[None, :]
    hits_cols = owner_cols[:, None] == node_ids[None, :]
    above = jnp.any(
        hits_rows[:, None, :, None] & ancestor[None, None, :, :] & hits_cols[None, :, None, :],
        axis=(2, 3),
    )
    tile_hits = mine_rows[:, None] == jnp.arange(tile_count, dtype=jnp.int32)[None, :]
    flagged = jnp.any(
        tile_hits[:, None, None, :]
        & hits_cols[None, :, :, None]
        & (row_blocks == 1)[None, None, :, :],
        axis=(2, 3),
    )
    diagonal = owner_rows[:, None] == owner_cols[None, :]
    linked = above & flagged
    correction = jnp.zeros(right_sides.shape, jnp.float32)
    forward = jnp.zeros(right_sides.shape, jnp.float32)
    forward_cols = jnp.zeros((rhs_count, col_tiles, tile_rows), jnp.float32)
    for height in range(LEVELS - 1, -1, -1):
        at_rows = depth_rows == height
        at_cols = depth_cols == height
        current = (right_sides - correction).astype(jnp.bfloat16)
        solve_weights = (diagonal & at_rows[:, None]).astype(jnp.float32)
        solved = sum_rows(rows_from_columns(factor, to_columns(current), solve_weights))
        forward = forward + solved
        solved_cols = to_columns(solved.astype(jnp.bfloat16))
        forward_cols = forward_cols + solved_cols.astype(jnp.float32)
        if height > 0:
            update_weights = (linked & at_cols[None, :]).astype(jnp.float32)
            correction = correction + sum_rows(
                rows_from_columns(factor, solved_cols, update_weights)
            )
    solution = jnp.zeros((rhs_count, col_tiles, tile_rows), jnp.float32)
    correction_cols = jnp.zeros((rhs_count, col_tiles, tile_rows), jnp.float32)
    for height in range(LEVELS):
        at_rows = depth_rows == height
        at_cols = depth_cols == height
        if height == 0:
            current = forward.astype(jnp.bfloat16)
        else:
            current = to_rows((forward_cols - correction_cols).astype(jnp.bfloat16))
        solve_weights = (diagonal & at_cols[None, :]).astype(jnp.float32)
        solved = sum_cols(columns_from_rows(factor, current, solve_weights))
        solution = solution + solved
        if height < LEVELS - 1:
            solved_rows = to_rows(solved.astype(jnp.bfloat16))
            update_weights = (linked & at_rows[:, None]).astype(jnp.float32)
            correction_cols = correction_cols + sum_cols(
                columns_from_rows(factor, solved_rows, update_weights)
            )
    return (forward, solution)


def solution(mesh):
    in_specs = (P(None, None, "prow"), P(None, "prow", None, "pcol"), P(), P())
    out_specs = (P(None, None, "prow"), P(None, None, "pcol"))
    return jax.shard_map(shards, mesh=mesh, in_specs=in_specs, out_specs=out_specs, check_vma=False)
```

profile of v0, /device:TPU:0, one launch (start us, length us, event | category | flops | bytes accessed | tf_op | source)
XLA Modules:
  0.0 793.3 jit_solution(14260200867232302940)
XLA Ops:
  9.5 1.3 select_reduce_fusion.2
  14.7 43.8 %all_gather.30 = bf16[32,16,256]{2,0,1:T(8,128)(2,1)S(1)} all-gather(bf16[32,1,256]{2,0,1:T(8,128)(2,1)S(1)} %copy.112), channel_id=1, replica_groups=mesh['prow'=16,'pcol'=2] {'prow'}, dimensions={1}, use_global_device_ids=true | all-gather | bytes 278528 | tf_op jit(solution)/shard_map/all_gather | solution.py:51
  59.2 3.4 psum.70
  62.6 36.9 %all_gather.31 = bf16[32,16,256]{2,0,1:T(8,128)(2,1)S(1)} all-gather(bf16[32,1,256]{2,0,1:T(8,128)(2,1)S(1)} %convert_element_type.179), channel_id=1, replica_groups=mesh['prow'=16,'pcol'=2] {'prow'}, dimensions={1}, use_global_device_ids=true | all-gather | bytes 278528 | tf_op jit(solution)/shard_map/all_gather | solution.py:51
  99.9 3.4 psum.71
  103.3 38.9 %all_gather.32 = bf16[32,16,256]{2,0,1:T(8,128)(2,1)S(1)} all-gather(bf16[32,1,256]{2,0,1:T(8,128)(2,1)S(1)} %subtract_convert_fusion.2), channel_id=1, replica_groups=mesh['prow'=16,'pcol'=2] {'prow'}, dimensions={1}, use_global_device_ids=true | all-gather | bytes 278528 | tf_op jit(solution)/shard_map/all_gather | solution.py:51
  142.6 3.4 psum.72
  146.1 36.9 %all_gather.33 = bf16[32,16,256]{2,0,1:T(8,128)(2,1)S(1)} all-gather(bf16[32,1,256]{2,0,1:T(8,128)(2,1)S(1)} %convert_element_type.183), channel_id=1, replica_groups=mesh['prow'=16,'pcol'=2] {'prow'}, dimensions={1}, use_global_device_ids=true | all-gather | bytes 278528 | tf_op jit(solution)/shard_map/all_gather | solution.py:51
  183.4 3.4 psum.73
  186.8 39.0 %all_gather.34 = bf16[32,16,256]{2,0,1:T(8,128)(2,1)S(1)} all-gather(bf16[32,1,256]{2,0,1:T(8,128)(2,1)S(1)} %subtract_convert_fusion.1), channel_id=1, replica_groups=mesh['prow'=16,'pcol'=2] {'prow'}, dimensions={1}, use_global_device_ids=true | all-gather | bytes 278528 | tf_op jit(solution)/shard_map/all_gather | solution.py:51
  226.2 3.4 psum.74
  229.6 1.0 convolution_multiply_fusion.4
  230.7 104.0 %all-reduce.6.cloned.1.call-done = f32[32,8,256]{2,0,1:T(8,128)} async-done(((f32[32,8,256]{2,0,1:T(8,128)}), f32[32,8,256]{2,0,1:T(8,128)}) %all-reduce.6.cloned.1.call-update) | async-done | bytes 262160 | tf_op jit(solution)/shard_map/psum | solution.py:75
  335.5 1.8 all_gather.36
  337.3 1.0 convolution_multiply_fusion.3
  338.3 40.2 %all_gather.35 = bf16[32,16,256]{2,0,1:T(8,128)(2,1)S(1)} all-gather(bf16[32,1,256]{2,0,1:T(8,128)(2,1)S(1)} %get-tuple-element.14), channel_id=1, replica_groups=mesh['prow'=16,'pcol'=2] {'prow'}, dimensions={1}, use_global_device_ids=true | all-gather | bytes 278528 | tf_op jit(solution)/shard_map/all_gather | solution.py:51
  378.6 68.9 %all-reduce.8.cloned.1.call-done = f32[32,8,256]{2,0,1:T(8,128)} async-done(((f32[32,8,256]{2,0,1:T(8,128)}), f32[32,8,256]{2,0,1:T(8,128)}) %all-reduce.8.cloned.1.call-update) | async-done | bytes 262160 | tf_op jit(solution)/shard_map/psum | solution.py:75
  448.3 1.8 all_gather.37
  451.2 108.9 %all-reduce.10.cloned.1.call-done = f32[32,8,256]{2,0,1:T(8,128)} async-done(((f32[32,8,256]{2,0,1:T(8,128)}), f32[32,8,256]{2,0,1:T(8,128)}) %all-reduce.10.cloned.1.call-update) | async-done | bytes 262160 | tf_op jit(solution)/shard_map/psum | solution.py:75
  560.8 1.8 all_gather.38
  563.7 108.7 %all-reduce.12.cloned.1.call-done = f32[32,8,256]{2,0,1:T(8,128)} async-done(((f32[32,8,256]{2,0,1:T(8,128)}), f32[32,8,256]{2,0,1:T(8,128)}) %all-reduce.12.cloned.1.call-update) | async-done | bytes 262160 | tf_op jit(solution)/shard_map/psum | solution.py:75
  673.3 1.8 all_gather.39
  676.8 108.1 %all-reduce.14.cloned.1.call-done = f32[32,8,256]{2,0,1:T(8,128)} async-done(((f32[32,8,256]{2,0,1:T(8,128)}), f32[32,8,256]{2,0,1:T(8,128)}) %all-reduce.14.cloned.1.call-update) | async-done | bytes 262160 | tf_op jit(solution)/shard_map/psum | solution.py:75
  784.9 1.0 add_add_fusion
  (59 shorter events, 14.5 us)
Async XLA Ops:
  7.2 51.5 %copy-start = (bf16[1,256,8,256]{3,2,1,0:T(8,128)(2,1)S(1)}, bf16[1,256,8,256]{3,2,1,0:T(8,128)(2,1)}, u32[]{:S(2)}) copy-start(bf16[1,256,8,256]{3,2,1,0:T(8,128)(2,1)} %param.5) | copy-start | bytes 3145732
  7.2 7.5 copy-start.3
  7.2 327.5 %all-reduce.6.cloned.1.call-start = ((), (), s32[]{:S(2)}) async-start(), calls=%async_computation | async-start | bytes 524288 | tf_op jit(solution)/shard_map/psum | solution.py:75
  12.7 0.7 copy-start.4
  230.6 216.9 %all-reduce.8.cloned.1.call-start = ((), (), s32[]{:S(2)}) async-start(), calls=%async_computation.1 | async-start | bytes 524288 | tf_op jit(solution)/shard_map/psum | solution.py:75
  338.3 221.8 %all-reduce.10.cloned.1.call-start = ((), (), s32[]{:S(2)}) async-start(), calls=%async_computation.2 | async-start | bytes 524288 | tf_op jit(solution)/shard_map/psum | solution.py:75
  451.1 221.4 %all-reduce.12.cloned.1.call-start = ((), (), s32[]{:S(2)}) async-start(), calls=%async_computation.3 | async-start | bytes 524288 | tf_op jit(solution)/shard_map/psum | solution.py:75
  563.7 221.2 %all-reduce.14.cloned.1.call-start = ((), (), s32[]{:S(2)}) async-start(), calls=%async_computation.4 | async-start | bytes 524288 | tf_op jit(solution)/shard_map/psum | solution.py:75
  675.1 109.8 %copy-start.2 = (f32[32,8,256]{2,0,1:T(8,128)S(1)}, f32[32,8,256]{2,0,1:T(8,128)}, u32[]{:S(2)}) copy-start(f32[32,8,256]{2,0,1:T(8,128)} %all-reduce.10.cloned.1.call-done) | copy-start | bytes 786436
  676.1 108.8 %copy-start.1 = (f32[32,8,256]{2,0,1:T(8,128)S(1)}, f32[32,8,256]{2,0,1:T(8,128)}, u32[]{:S(2)}) copy-start(f32[32,8,256]{2,0,1:T(8,128)} %all-reduce.6.cloned.1.call-done) | copy-start | bytes 786436
Sparse Core Ops, SparseCore 0:
  230.8 103.9 all-reduce.5
  340.5 106.9 all-reduce.7
  453.3 106.7 all-reduce.9
  565.7 106.6 all-reduce.11
  678.1 106.7 all-reduce.13
where the time goes:
time: 794 us; the launch traced here: 793 us
  waiting for transfers between devices  499 us (63%)
  blocking collectives  260 us (33%)
  between operations  16 us (2%)
    psum x5, waiting for transfers between devices, sum_cols(): return lax.psum(partial_value, 'prow')  499 us
    all_gather x6, blocking collectives, to_columns(): collected = lax.all_gather(vector, 'prow', axis=1, tiled=True)  236 us
    psum x5, blocking collectives, sum_rows(): return lax.psum(partial_value, 'pcol')  17 us
  transfers between devices with their start and end apart: 5, of which 5 were waited for; matrix products, arithmetic and copies ran while one was open for 0% of the time, Pallas kernels for 0%

commit v1 on v0

--- a/solution.py
+++ b/solution.py
@@ -48,7 +48,15 @@
     row_groups = row_count // col_count
     col_index = lax.axis_index("pcol")
     rhs_count, row_tiles, tile_rows = vector.shape
-    collected = lax.all_gather(vector, "prow", axis=1, tiled=True)
+    ways, here, step = (lax.axis_size("prow"), lax.axis_index("prow"), vector.shape[1])
+    line, have = (vector, 1)
+    while have < ways:
+        line = jnp.concatenate(
+            [line, lax.ppermute(line, "prow", [(d, (d - have) % ways) for d in range(ways)])],
+            axis=1,
+        )
+        have = 2 * have
+    collected = jnp.roll(line, here * step, axis=1)
     collected = collected.reshape(rhs_count, row_groups, col_count, row_tiles, tile_rows)
     picked = lax.dynamic_index_in_dim(collected, col_index, 2, keepdims=False)
     return jnp.transpose(picked, (0, 2, 1, 3)).reshape(rhs_count, row_tiles * row_groups, tile_rows)

time: 794 us -> 734 us (0.924)
  blocking collectives: 260 us -> 24.3 us
  waiting for transfers between devices: 499 us -> 612 us
  starting transfers between devices: 0.2 us -> 60.7 us
    all_gather x6 -> x0, blocking collectives: 236 us -> none  [to_columns(): collected = lax.all_gather(vector, 'prow', axis=1, tiled=True)]
    ppermute x0 -> x24, waiting for transfers between devices: none -> 81.5 us  [to_columns(): lax.ppermute(line, 'prow', [(d, (d - have) % ways) for d in range(ways)])]
    ppermute x0 -> x24, starting transfers between devices: none -> 60.5 us  [to_columns(): lax.ppermute(line, 'prow', [(d, (d - have) % ways) for d in range(ways)])]
    psum x5, waiting for transfers between devices: 499 us -> 530 us  [sum_cols(): return lax.psum(partial_value, 'prow')]
  transfers between devices with their start and end apart: 5 -> 29, of which waited for: 5 -> 27; matrix products, arithmetic and copies ran while one was open for 0% -> 1% of each run, Pallas kernels for 0% -> 0%
where the time goes in v1:
time: 734 us
  waiting for transfers between devices  612 us (83%)
  starting transfers between devices  60.7 us (8%)
  blocking collectives  24.3 us (3%)
  between operations  16.3 us (2%)
  other arithmetic  8 us (1%)
    psum x5, waiting for transfers between devices, sum_cols(): return lax.psum(partial_value, 'prow')  530 us
    ppermute x24, waiting for transfers between devices, to_columns(): lax.ppermute(line, 'prow', [(d, (d - have) % ways) for d in range(ways)])  81.5 us
    ppermute x24, starting transfers between devices, to_columns(): lax.ppermute(line, 'prow', [(d, (d - have) % ways) for d in range(ways)])  60.5 us
    psum x5, blocking collectives, sum_rows(): return lax.psum(partial_value, 'pcol')  17 us
  transfers between devices with their start and end apart: 29, of which 27 were waited for; matrix products, arithmetic and copies ran while one was open for 1% of the time, Pallas kernels for 0%

profile of v1, /device:TPU:0, one launch (start us, length us, event | category | flops | bytes accessed | tf_op | source)
XLA Modules:
  0.0 733.7 jit_solution(290813934964556367)
XLA Ops:
  8.1 7.0 collective-permute-start
  27.1 3.8 collective-permute-done.2
  31.0 6.8 collective-permute-done.3
  41.9 4.8 collective-permute-start.4
  52.9 3.6 collective-permute-done.6
  56.6 7.2 collective-permute-done.7
  67.9 9.4 %collective-permute-start.8 = (bf16[32,1,256]{2,0,1:T(8,128)(2,1)S(1)}, bf16[32,1,256]{2,0,1:T(8,128)(2,1)S(1)}, u32[]{:S(2)}, u32[]{:S(2)}) collective-permute-start(bf16[32,1,256]{2,0,1:T(8,128)(2,1)S(1)} %get-tuple-element.22), channel_id=1, source_target_pairs={{0,30},{2,0},{4,2},{6,4},{8,6},{10,8},{12,10},{14,12},{16,14},{18,... | collective-permute-start | bytes 49160 | tf_op jit(solution)/shard_map/ppermute | solution.py:55
  82.8 4.2 collective-permute-done.10
  87.1 6.3 collective-permute-done.11
  97.5 10.4 %collective-permute-start.12 = (bf16[32,1,256]{2,0,1:T(8,128)(2,1)S(1)}, bf16[32,1,256]{2,0,1:T(8,128)(2,1)S(1)}, u32[]{:S(2)}, u32[]{:S(2)}) collective-permute-start(bf16[32,1,256]{2,0,1:T(8,128)(2,1)S(1)} %get-tuple-element.20), channel_id=1, source_target_pairs={{0,30},{2,0},{4,2},{6,4},{8,6},{10,8},{12,10},{14,12},{16,14},{18,... | collective-permute-start | bytes 49160 | tf_op jit(solution)/shard_map/ppermute | solution.py:55
  113.4 4.2 collective-permute-done.14
  117.7 6.3 collective-permute-done.15
  124.7 3.4 psum.73
  128.1 10.4 %collective-permute-start.16 = (bf16[32,1,256]{2,0,1:T(8,128)(2,1)S(1)}, bf16[32,1,256]{2,0,1:T(8,128)(2,1)S(1)}, u32[]{:S(2)}, u32[]{:S(2)}) collective-permute-start(bf16[32,1,256]{2,0,1:T(8,128)(2,1)S(1)} %get-tuple-element.18), channel_id=1, source_target_pairs={{0,30},{2,0},{4,2},{6,4},{8,6},{10,8},{12,10},{14,12},{16,14},{18,... | collective-permute-start | bytes 49160 | tf_op jit(solution)/shard_map/ppermute | solution.py:55
  144.0 4.2 collective-permute-done.18
  148.3 6.3 collective-permute-done.19
  155.3 3.4 psum.74
  158.7 10.4 %collective-permute-start.20 = (bf16[32,1,256]{2,0,1:T(8,128)(2,1)S(1)}, bf16[32,1,256]{2,0,1:T(8,128)(2,1)S(1)}, u32[]{:S(2)}, u32[]{:S(2)}) collective-permute-start(bf16[32,1,256]{2,0,1:T(8,128)(2,1)S(1)} %get-tuple-element.12), channel_id=1, source_target_pairs={{0,30},{2,0},{4,2},{6,4},{8,6},{10,8},{12,10},{14,12},{16,14},{18,... | collective-permute-start | bytes 49160 | tf_op jit(solution)/shard_map/ppermute | solution.py:55
  174.8 4.5 collective-permute-done.22
  179.4 96.0 %all-reduce.6.cloned.1.call-done = f32[32,8,256]{2,0,1:T(8,128)} async-done(((f32[32,8,256]{2,0,1:T(8,128)}), f32[32,8,256]{2,0,1:T(8,128)}) %all-reduce.6.cloned.1.call-update) | async-done | bytes 262160 | tf_op jit(solution)/shard_map/psum | solution.py:83
  279.3 108.6 %all-reduce.8.cloned.1.call-done = f32[32,8,256]{2,0,1:T(8,128)} async-done(((f32[32,8,256]{2,0,1:T(8,128)}), f32[32,8,256]{2,0,1:T(8,128)}) %all-reduce.8.cloned.1.call-update) | async-done | bytes 262160 | tf_op jit(solution)/shard_map/psum | solution.py:83
  391.6 108.9 %all-reduce.10.cloned.1.call-done = f32[32,8,256]{2,0,1:T(8,128)} async-done(((f32[32,8,256]{2,0,1:T(8,128)}), f32[32,8,256]{2,0,1:T(8,128)}) %all-reduce.10.cloned.1.call-update) | async-done | bytes 262160 | tf_op jit(solution)/shard_map/psum | solution.py:83
  504.1 108.7 %all-reduce.12.cloned.1.call-done = f32[32,8,256]{2,0,1:T(8,128)} async-done(((f32[32,8,256]{2,0,1:T(8,128)}), f32[32,8,256]{2,0,1:T(8,128)}) %all-reduce.12.cloned.1.call-update) | async-done | bytes 262160 | tf_op jit(solution)/shard_map/psum | solution.py:83
  617.2 108.1 %all-reduce.14.cloned.1.call-done = f32[32,8,256]{2,0,1:T(8,128)} async-done(((f32[32,8,256]{2,0,1:T(8,128)}), f32[32,8,256]{2,0,1:T(8,128)}) %all-reduce.14.cloned.1.call-update) | async-done | bytes 262160 | tf_op jit(solution)/shard_map/psum | solution.py:83
  (152 shorter events, 70.1 us)
Async XLA Ops:
  7.2 268.2 %all-reduce.6.cloned.1.call-start = ((), (), s32[]{:S(2)}) async-start(), calls=%async_computation | async-start | bytes 524288 | tf_op jit(solution)/shard_map/psum | solution.py:83
  8.1 14.5 %collective-permute-start = (bf16[32,1,256]{2,0,1:T(8,128)(2,1)S(1)}, bf16[32,1,256]{2,0,1:T(8,128)(2,1)S(1)}, u32[]{:S(2)}, u32[]{:S(2)}) collective-permute-start(bf16[32,1,256]{2,0,1:T(8,128)(2,1)S(1)} %get-tuple-element.26), channel_id=1, source_target_pairs={{0,30},{2,0},{4,2},{6,4},{8,6},{10,8},{12,10},{14,12},{16,14},{18,... | collective-permute-start | bytes 49160 | tf_op jit(solution)/shard_map/ppermute | solution.py:55
  26.6 4.3 collective-permute-start.2
  30.9 6.9 collective-permute-start.3
  41.9 6.3 collective-permute-start.4
  52.2 4.3 collective-permute-start.6
  56.5 7.3 collective-permute-start.7
  67.9 10.8 %collective-permute-start.8 = (bf16[32,1,256]{2,0,1:T(8,128)(2,1)S(1)}, bf16[32,1,256]{2,0,1:T(8,128)(2,1)S(1)}, u32[]{:S(2)}, u32[]{:S(2)}) collective-permute-start(bf16[32,1,256]{2,0,1:T(8,128)(2,1)S(1)} %get-tuple-element.22), channel_id=1, source_target_pairs={{0,30},{2,0},{4,2},{6,4},{8,6},{10,8},{12,10},{14,12},{16,14},{18,... | collective-permute-start | bytes 49160 | tf_op jit(solution)/shard_map/ppermute | solution.py:55
  82.7 4.3 collective-permute-start.10
  87.0 6.4 collective-permute-start.11
  97.5 11.9 %collective-permute-start.12 = (bf16[32,1,256]{2,0,1:T(8,128)(2,1)S(1)}, bf16[32,1,256]{2,0,1:T(8,128)(2,1)S(1)}, u32[]{:S(2)}, u32[]{:S(2)}) collective-permute-start(bf16[32,1,256]{2,0,1:T(8,128)(2,1)S(1)} %get-tuple-element.20), channel_id=1, source_target_pairs={{0,30},{2,0},{4,2},{6,4},{8,6},{10,8},{12,10},{14,12},{16,14},{18,... | collective-permute-start | bytes 49160 | tf_op jit(solution)/shard_map/ppermute | solution.py:55
  113.3 4.3 collective-permute-start.14
  117.6 6.4 collective-permute-start.15
  128.1 11.9 %collective-permute-start.16 = (bf16[32,1,256]{2,0,1:T(8,128)(2,1)S(1)}, bf16[32,1,256]{2,0,1:T(8,128)(2,1)S(1)}, u32[]{:S(2)}, u32[]{:S(2)}) collective-permute-start(bf16[32,1,256]{2,0,1:T(8,128)(2,1)S(1)} %get-tuple-element.18), channel_id=1, source_target_pairs={{0,30},{2,0},{4,2},{6,4},{8,6},{10,8},{12,10},{14,12},{16,14},{18,... | collective-permute-start | bytes 49160 | tf_op jit(solution)/shard_map/ppermute | solution.py:55
  143.9 4.3 collective-permute-start.18
  148.2 6.4 collective-permute-start.19
  158.7 11.9 %collective-permute-start.20 = (bf16[32,1,256]{2,0,1:T(8,128)(2,1)S(1)}, bf16[32,1,256]{2,0,1:T(8,128)(2,1)S(1)}, u32[]{:S(2)}, u32[]{:S(2)}) collective-permute-start(bf16[32,1,256]{2,0,1:T(8,128)(2,1)S(1)} %get-tuple-element.12), channel_id=1, source_target_pairs={{0,30},{2,0},{4,2},{6,4},{8,6},{10,8},{12,10},{14,12},{16,14},{18,... | collective-permute-start | bytes 49160 | tf_op jit(solution)/shard_map/ppermute | solution.py:55
  170.2 217.8 %all-reduce.8.cloned.1.call-start = ((), (), s32[]{:S(2)}) async-start(), calls=%async_computation.1 | async-start | bytes 524288 | tf_op jit(solution)/shard_map/psum | solution.py:83
  170.6 4.1 collective-permute-start.21
  174.7 4.6 collective-permute-start.22
  179.3 99.7 %collective-permute-start.23 = (bf16[32,8,256]{2,0,1:T(8,128)(2,1)S(1)}, bf16[32,8,256]{2,0,1:T(8,128)(2,1)S(1)}, u32[]{:S(2)}, u32[]{:S(2)}) collective-permute-start(bf16[32,8,256]{2,0,1:T(8,128)(2,1)S(1)} %pad_maximum_fusion.5), channel_id=1, source_target_pairs={{0,16},{2,18},{4,20},{6,22},{8,24},{10,26},{12,28},{14,30},{16,0},... | collective-permute-start | bytes 393224 | tf_op jit(solution)/shard_map/ppermute | solution.py:55
  279.0 221.5 %all-reduce.10.cloned.1.call-start = ((), (), s32[]{:S(2)}) async-start(), calls=%async_computation.2 | async-start | bytes 524288 | tf_op jit(solution)/shard_map/psum | solution.py:83
  391.5 221.4 %all-reduce.12.cloned.1.call-start = ((), (), s32[]{:S(2)}) async-start(), calls=%async_computation.3 | async-start | bytes 524288 | tf_op jit(solution)/shard_map/psum | solution.py:83
  504.1 221.2 %all-reduce.14.cloned.1.call-start = ((), (), s32[]{:S(2)}) async-start(), calls=%async_computation.4 | async-start | bytes 524288 | tf_op jit(solution)/shard_map/psum | solution.py:83
  (11 other events, 273.9 us)
Sparse Core Ops, SparseCore 0:
  170.3 105.0 all-reduce.5
  281.2 106.6 all-reduce.7
  393.7 106.7 all-reduce.9
  506.1 106.6 all-reduce.11
  618.5 106.7 all-reduce.13
